TPU v7x, 32 devices: a whole 2x2x4 slice. The times are simulated.
32 devices in a mesh: layer: 8 (over y, x, core), dp: 4 (over z).
Axes of the slice: x: 2, y: 2, z: 4, core: 2. Of those that a mesh axis runs over, the one named last changes fastest.
Arguments:
- resid_in: bfloat16 [4, 128, 3584], P(None, 'dp'), may hold values from -6 to 6
- resid_out: bfloat16 [4, 128, 3584], P(None, ('layer', 'dp')), may hold values from -4 to 4
- encoder: bfloat16 [2, 3584, 32768], P(None, None, ('layer', 'dp')), may hold values from -0.09375 to 0.09375
- enc_bias: float32 [2, 32768], P(None, ('layer', 'dp')), may hold values from -3 to 3
- decoder: bfloat16 [5, 32768, 3584], P(None, ('layer', 'dp')), may hold values from -0.046875 to 0.046875
- active: int32 [4, 4, 32], replicated, may hold values from 0 to 127, all different within a row
Outputs:
- recon: bfloat16 [4, 128, 3584], P(None, ('layer', 'dp'))
- grad_encoder: bfloat16 [2, 3584, 32768], P(None, None, ('layer', 'dp'))
- grad_bias: float32 [2, 32768], P(None, ('layer', 'dp'))
- grad_decoder: bfloat16 [5, 32768, 3584], P(None, ('layer', 'dp'))
Inputs may be any that keep to these rules, and one draw needn't show every extreme that they name: Row active[l, n] lists 32 different blocks of layer l, active for tokens n * 32 to (n + 1) * 32 - 1; every block number appears in at least one row of active, counting the rows of all layers together (not necessarily in a row of every layer).
All inputs are finite; a program needn't handle non-finite values.
Results may differ from a plain program's by a relative error of at most 0.0059.
Values may be sent and summed in bfloat16 or wider, within the bound.
A program may use at most 192 MiB of HBM per device.

v0:
```python
import jax
import jax.numpy as jnp
from jax import lax
from jax.sharding import PartitionSpec as P

FEAT = 16384
BLOCK = 128
LAYERS = 4


def per_device(resid_in, resid_out, encoder, enc_bias, decoder, active):
    tok_dev = resid_in.shape[1]
    model_width = resid_in.shape[2]
    local_width = encoder.shape[2]
    dp_count = lax.axis_size("dp")
    all_count = lax.axis_size("layer") * dp_count
    device_rank = lax.axis_index("layer") * dp_count + lax.axis_index("dp")
    first_column = device_rank * local_width
    fold_side = first_column // FEAT
    offset = first_column - fold_side * FEAT
    targets = lax.all_gather(resid_out, ("layer", "dp"), axis=1, tiled=True)
    layer_ids = [fold_side, LAYERS - 1 - fold_side]
    picked = jnp.stack(
        [lax.dynamic_index_in_dim(resid_in, layer_id, 0, keepdims=False) for layer_id in layer_ids]
    )
    inputs = lax.all_gather(picked, "dp", axis=1, tiled=True)
    tokens = inputs.shape[1]
    pre_acts = (
        jnp.einsum("krd,kdf->krf", inputs, encoder, preferred_element_type=jnp.float32)
        + enc_bias[:, None, :]
    )
    block_ids = offset // BLOCK + jnp.arange(local_width // BLOCK, dtype=jnp.int32)
    block_masks = []
    for layer_id in layer_ids:
        listed = lax.dynamic_index_in_dim(active, layer_id, 0, keepdims=False)
        listed_hit = jnp.any(listed[:, :, None] == block_ids[None, None, :], axis=1).astype(
            jnp.float32
        )
        spread = jnp.broadcast_to(
            listed_hit[:, None, :, None], (listed_hit.shape[0], tok_dev, listed_hit.shape[1], BLOCK)
        )
        block_masks.append(spread.reshape(tokens, local_width))
    block_keep = jnp.stack(block_masks)
    positive = jnp.maximum(pre_acts, 0.0)
    feature_codes = (block_keep * positive * positive).astype(jnp.bfloat16)
    pair_table = []
    for pair_slot in range(decoder.shape[0]):
        second = pair_slot >= LAYERS - fold_side
        pair_table.append(
            (second.astype(jnp.int32), jnp.where(second, pair_slot - 1, fold_side + pair_slot))
        )
    decoded = jnp.zeros((LAYERS, tokens, model_width), jnp.float32)
    for pair_slot in range(decoder.shape[0]):
        source_slot, target_layer = pair_table[pair_slot]
        source_codes = lax.dynamic_index_in_dim(feature_codes, source_slot, 0, keepdims=False)
        decoded_part = jnp.dot(source_codes, decoder[pair_slot], preferred_element_type=jnp.float32)
        current = lax.dynamic_index_in_dim(decoded, target_layer, 0, keepdims=False)
        decoded = lax.dynamic_update_index_in_dim(decoded, current + decoded_part, target_layer, 0)
    totals = lax.psum(decoded, ("layer", "dp"))
    share = tokens // all_count
    recon = lax.dynamic_slice_in_dim(totals, device_rank * share, share, 1).astype(jnp.bfloat16)
    errors_all = (totals - targets.astype(jnp.float32)).astype(jnp.bfloat16)
    grad_parts = []
    back_codes = jnp.zeros((2, tokens, local_width), jnp.float32)
    for pair_slot in range(decoder.shape[0]):
        source_slot, target_layer = pair_table[pair_slot]
        source_codes = lax.dynamic_index_in_dim(feature_codes, source_slot, 0, keepdims=False)
        target_errors = lax.dynamic_index_in_dim(errors_all, target_layer, 0, keepdims=False)
        grad_parts.append(
            lax.dot_general(
                source_codes,
                target_errors,
                (((0,), (0,)), ((), ())),
                preferred_element_type=jnp.float32,
            ).astype(jnp.bfloat16)
        )
        pulled = lax.dot_general(
            target_errors,
            decoder[pair_slot],
            (((1,), (1,)), ((), ())),
            preferred_element_type=jnp.float32,
        )
        current = lax.dynamic_index_in_dim(back_codes, source_slot, 0, keepdims=False)
        back_codes = lax.dynamic_update_index_in_dim(back_codes, current + pulled, source_slot, 0)
    grad_decoder = jnp.stack(grad_parts)
    back_pre = (back_codes * block_keep * (2.0 * positive)).astype(jnp.bfloat16)
    grad_encoder = jnp.einsum(
        "krd,krf->kdf", inputs, back_pre, preferred_element_type=jnp.float32
    ).astype(jnp.bfloat16)
    grad_bias = jnp.sum(back_pre.astype(jnp.float32), axis=1)
    return (recon, grad_encoder, grad_bias, grad_decoder)


def solution(mesh):
    in_specs = (
        P(None, "dp", None),
        P(None, ("layer", "dp"), None),
        P(None, None, ("layer", "dp")),
        P(None, ("layer", "dp")),
        P(None, ("layer", "dp"), None),
        P(),
    )
    out_specs = (
        P(None, ("layer", "dp"), None),
        P(None, None, ("layer", "dp")),
        P(None, ("layer", "dp")),
        P(None, ("layer", "dp"), None),
    )
    return jax.shard_map(
        per_device, mesh=mesh, in_specs=in_specs, out_specs=out_specs, check_vma=False
    )
```

profile of v0, /device:TPU:0, one launch (start us, length us, event | category | flops | bytes accessed | tf_op | source)
XLA Modules:
  0.0 404.9 jit_solution(1773918791542335406)
XLA Ops:
  7.2 0.0 copy-start.2
  7.2 0.0 all-gather.3.cloned.1.call-start
  7.3 1.1 constant_dynamic-slice_fusion.9
  8.3 0.8 pad_maximum_fusion
  9.1 0.0 all-gather.3.cloned.1.call-update
  9.2 0.0 all-reduce.2.cloned.1.call-start
  9.3 0.7 fusion.171
  10.0 0.3 compare_reduce_fusion
  10.3 0.1 broadcast_in_dim.53
  10.4 0.1 stack_reshape.6
  10.5 0.1 broadcast_in_dim.54
  10.6 0.1 stack_reshape.7
  10.9 43.4 %all-gather.3.cloned.1.call-done = bf16[2,128,3584]{2,1,0:T(8,128)(2,1)} async-done(((bf16[2,32,3584]{2,1,0:T(8,128)(2,1)}), bf16[2,128,3584]{2,1,0:T(8,128)(2,1)}) %all-gather.3.cloned.1.call-update) | async-done | bytes 1835024 | tf_op jit(solution)/shard_map/all_gather | solution.py:26
  54.2 0.0 copy-done.2
  54.2 8.0 %fusion.115 = (bf16[2,128,1024]{2,1,0:T(8,128)(2,1)S(1)}, f32[2,128,1024]{2,1,0:T(8,128)S(1)}) fusion(f32[2,128,1024]{2,1,0:T(8,128)S(1)} %constant_dynamic-update-slice_fusion, f32[2,1024]{1,0:T(2,128)S(1)} %copy-done.2, bf16[2,128,3584]{2,1,0:T(8,128)(2,1)} %all-gather.3.cloned.1.call-done, bf16[2,3584,1024]{2,1,0:T(8,128)(2,1)} %param.8), kind=kOutput, calls=%fused_computation.73 | convolution fusion | flops 1880358912 | bytes 19144704 | tf_op jit(solution)/shard_map/krd,kdf->krf/dot_general | solution.py:29
  62.2 3.9 broadcast_in_dim.52
  66.1 5.4 %fusion.33 = f32[4,128,3584]{2,1,0:T(8,128)} fusion(f32[4,128,3584]{2,1,0:T(8,128)} %broadcast_in_dim.52, s32[]{:T(128)S(6)} %select_n.104, bf16[5,1024,3584]{2,1,0:T(8,128)(2,1)} %param.10, bf16[2,128,1024]{2,1,0:T(8,128)(2,1)S(1)} %get-tuple-element.16, s32[]{:T(128)S(6)} %select_n.102), kind=kOutput, calls=%fused_computation.43 | convolution fusion | flops 939524096 | bytes 9437192 | tf_op jit(solution)/shard_map/dot_general | solution.py:56
  71.6 1.6 constant_dynamic-slice_fusion.7
  73.2 5.5 %fusion.42 = f32[4,128,3584]{2,1,0:T(8,128)} fusion(f32[4,128,3584]{2,1,0:T(8,128)} %fusion.33, s32[]{:T(128)S(6)} %select_n.106, bf16[5,1024,3584]{2,1,0:T(8,128)(2,1)} %param.10, f32[1,128,3584]{2,1,0:T(8,128)S(1)} %constant_dynamic-slice_fusion.7, bf16[2,128,1024]{2,1,0:T(8,128)(2,1)S(1)} %get-tuple-element.16, s32[]{:T(128)S(6)} %select_n.107), kind=kOutput, calls=%fused_computation.46 | convolution fusion | flops 939982848 | bytes 11272200 | tf_op jit(solution)/shard_map/dot_general | solution.py:56
  78.7 1.6 constant_dynamic-slice_fusion.6
  80.3 5.5 %fusion.51 = f32[4,128,3584]{2,1,0:T(8,128)} fusion(f32[4,128,3584]{2,1,0:T(8,128)} %fusion.42, s32[]{:T(128)S(6)} %select_n.109, bf16[5,1024,3584]{2,1,0:T(8,128)(2,1)} %param.10, f32[1,128,3584]{2,1,0:T(8,128)S(1)} %constant_dynamic-slice_fusion.6, bf16[2,128,1024]{2,1,0:T(8,128)(2,1)S(1)} %get-tuple-element.16, s32[]{:T(128)S(6)} %select_n.110), kind=kOutput, calls=%fused_computation.49 | convolution fusion | flops 939982848 | bytes 11272200 | tf_op jit(solution)/shard_map/dot_general | solution.py:56
  85.8 1.6 constant_dynamic-slice_fusion.4
  87.4 5.5 %fusion.60 = f32[4,128,3584]{2,1,0:T(8,128)} fusion(f32[4,128,3584]{2,1,0:T(8,128)} %fusion.51, s32[]{:T(128)S(6)} %select_n.112, bf16[5,1024,3584]{2,1,0:T(8,128)(2,1)} %param.10, f32[1,128,3584]{2,1,0:T(8,128)S(1)} %constant_dynamic-slice_fusion.4, bf16[2,128,1024]{2,1,0:T(8,128)(2,1)S(1)} %get-tuple-element.16, s32[]{:T(128)S(6)} %select_n.113), kind=kOutput, calls=%fused_computation.52 | convolution fusion | flops 939982848 | bytes 11272200 | tf_op jit(solution)/shard_map/dot_general | solution.py:56
  92.9 1.6 constant_dynamic-slice_fusion.3
  94.5 0.0 copy-start.1
  94.5 5.5 %fusion.69 = f32[4,128,3584]{2,1,0:T(8,128)} fusion(f32[4,128,3584]{2,1,0:T(8,128)} %fusion.60, s32[]{:T(128)S(6)} %select_n.115, bf16[5,1024,3584]{2,1,0:T(8,128)(2,1)} %param.10, f32[1,128,3584]{2,1,0:T(8,128)S(1)} %constant_dynamic-slice_fusion.3, bf16[2,128,1024]{2,1,0:T(8,128)(2,1)S(1)} %get-tuple-element.16, s32[]{:T(128)S(6)} %select_n.116), kind=kOutput, calls=%fused_computation.55 | convolution fusion | flops 939982848 | bytes 11272200 | tf_op jit(solution)/shard_map/dot_general | solution.py:56
  100.0 0.0 all-reduce.2.cloned.1.call-update
  100.0 0.2 all-gather.5.cloned.1.call-start
  100.3 0.0 copy-done.1
  100.3 0.7 copy.19
  101.0 0.0 all-gather.5.cloned.1.call-update
  101.0 165.3 %all-reduce.2.cloned.1.call-done = f32[4,128,3584]{2,1,0:T(8,128)} async-done(((f32[4,128,3584]{2,1,0:T(8,128)}), f32[4,128,3584]{2,1,0:T(8,128)}) %all-reduce.2.cloned.1.call-update) | async-done | bytes 7340048 | tf_op jit(solution)/shard_map/psum | solution.py:59
  266.3 1.7 dynamic-slice_convert_fusion
  268.0 62.2 %all-gather.5.cloned.1.call-done = bf16[4,128,3584]{2,0,1:T(4,128)(2,1)} async-done(((bf16[4,4,3584]{2,0,1:T(4,128)(2,1)}), bf16[4,128,3584]{2,0,1:T(4,128)(2,1)}) %all-gather.5.cloned.1.call-update) | async-done | bytes 3670032 | tf_op jit(solution)/shard_map/all_gather | solution.py:21
  330.3 5.5 %subtract_convert_fusion = bf16[4,128,3584]{2,1,0:T(8,128)(2,1)S(1)} fusion(f32[4,128,3584]{2,1,0:T(8,128)} %all-reduce.2.cloned.1.call-done, bf16[4,128,3584]{2,0,1:T(4,128)(2,1)} %all-gather.5.cloned.1.call-done), kind=kLoop, calls=%fused_computation.31 | loop fusion | flops 5505024 | bytes 14680064 | tf_op jit(solution)/shard_map/convert_element_type | solution.py:62
  335.7 5.2 %bitcast_dynamic-update-slice_fusion.4 = bf16[5,1024,3584]{2,1,0:T(8,128)(2,1)} fusion(bf16[4,128,3584]{2,1,0:T(8,128)(2,1)S(1)} %subtract_convert_fusion, s32[]{:T(128)S(6)} %select_n.104, bf16[2,128,1024]{2,1,0:T(8,128)(2,1)S(1)} %get-tuple-element.16, s32[]{:T(128)S(6)} %select_n.102), kind=kOutput, calls=%fused_computation.10 | convolution fusion | flops 943194112 | bytes 8519688 | tf_op jit(solution)/shard_map/dot_general | solution.py:70
  340.9 5.1 %bitcast_dynamic-update-slice_fusion.3 = bf16[5,1024,3584]{2,1,0:T(8,128)(2,1)} fusion(bf16[5,1024,3584]{2,1,0:T(8,128)(2,1)} %bitcast_dynamic-update-slice_fusion.4, bf16[4,128,3584]{2,1,0:T(8,128)(2,1)S(1)} %subtract_convert_fusion, s32[]{:T(128)S(6)} %select_n.106, bf16[2,128,1024]{2,1,0:T(8,128)(2,1)S(1)} %get-tuple-element.16, s32[]{:T(128)S(6)} %select_n.107), kind=kOutput, calls=%fused_computation.9 | convolution fusion | flops 943194112 | bytes 8519688 | tf_op jit(solution)/shard_map/dot_general | solution.py:70
  346.0 5.1 %bitcast_dynamic-update-slice_fusion.2 = bf16[5,1024,3584]{2,1,0:T(8,128)(2,1)} fusion(bf16[5,1024,3584]{2,1,0:T(8,128)(2,1)} %bitcast_dynamic-update-slice_fusion.3, bf16[4,128,3584]{2,1,0:T(8,128)(2,1)S(1)} %subtract_convert_fusion, s32[]{:T(128)S(6)} %select_n.109, bf16[2,128,1024]{2,1,0:T(8,128)(2,1)S(1)} %get-tuple-element.16, s32[]{:T(128)S(6)} %select_n.110), kind=kOutput, calls=%fused_computation.8 | convolution fusion | flops 943194112 | bytes 8519688 | tf_op jit(solution)/shard_map/dot_general | solution.py:70
  351.2 5.1 %bitcast_dynamic-update-slice_fusion.1 = bf16[5,1024,3584]{2,1,0:T(8,128)(2,1)} fusion(bf16[5,1024,3584]{2,1,0:T(8,128)(2,1)} %bitcast_dynamic-update-slice_fusion.2, bf16[4,128,3584]{2,1,0:T(8,128)(2,1)S(1)} %subtract_convert_fusion, s32[]{:T(128)S(6)} %select_n.112, bf16[2,128,1024]{2,1,0:T(8,128)(2,1)S(1)} %get-tuple-element.16, s32[]{:T(128)S(6)} %select_n.113), kind=kOutput, calls=%fused_computation.7 | convolution fusion | flops 943194112 | bytes 8519688 | tf_op jit(solution)/shard_map/dot_general | solution.py:70
  356.3 5.1 %bitcast_dynamic-update-slice_fusion = bf16[5,1024,3584]{2,1,0:T(8,128)(2,1)} fusion(bf16[5,1024,3584]{2,1,0:T(8,128)(2,1)} %bitcast_dynamic-update-slice_fusion.1, bf16[4,128,3584]{2,1,0:T(8,128)(2,1)S(1)} %subtract_convert_fusion, s32[]{:T(128)S(6)} %select_n.115, bf16[2,128,1024]{2,1,0:T(8,128)(2,1)S(1)} %get-tuple-element.16, s32[]{:T(128)S(6)} %select_n.116), kind=kOutput, calls=%fused_computation.6 | convolution fusion | flops 943194112 | bytes 8519688 | tf_op jit(solution)/shard_map/dot_general | solution.py:70
  361.5 0.1 broadcast.16
  361.6 5.7 %fusion.76 = f32[2,128,1024]{2,1,0:T(8,128)S(1)} fusion(f32[2,128,1024]{2,1,0:T(8,128)S(1)} %broadcast.16, s32[]{:T(128)S(6)} %select_n.102, bf16[5,1024,3584]{2,1,0:T(8,128)(2,1)} %param.10, bf16[4,128,3584]{2,1,0:T(8,128)(2,1)S(1)} %subtract_convert_fusion, s32[]{:T(128)S(6)} %select_n.104), kind=kOutput, calls=%fused_computation.60 | convolution fusion | flops 939524096 | bytes 8781832 | tf_op jit(solution)/shard_map/dot_general | solution.py:77
  367.4 5.5 %fusion.85 = f32[2,128,1024]{2,1,0:T(8,128)S(1)} fusion(f32[2,128,1024]{2,1,0:T(8,128)S(1)} %fusion.76, s32[]{:T(128)S(6)} %select_n.107, bf16[5,1024,3584]{2,1,0:T(8,128)(2,1)} %param.10, bf16[4,128,3584]{2,1,0:T(8,128)(2,1)S(1)} %subtract_convert_fusion, s32[]{:T(128)S(6)} %select_n.106, f32[1,128,1024]{2,1,0:T(8,128)S(1)} %constant_dynamic-slice_fusion.2), kind=kOutput, calls=%fused_computation.63 | convolution fusion | flops 939655168 | bytes 9306120 | tf_op jit(solution)/shard_map/dot_general | solution.py:77
  373.0 5.5 %fusion.94 = f32[2,128,1024]{2,1,0:T(8,128)S(1)} fusion(f32[2,128,1024]{2,1,0:T(8,128)S(1)} %fusion.85, s32[]{:T(128)S(6)} %select_n.110, bf16[5,1024,3584]{2,1,0:T(8,128)(2,1)} %param.10, bf16[4,128,3584]{2,1,0:T(8,128)(2,1)S(1)} %subtract_convert_fusion, s32[]{:T(128)S(6)} %select_n.109, f32[1,128,1024]{2,1,0:T(8,128)S(1)} %constant_dynamic-slice_fusion.1), kind=kOutput, calls=%fused_computation.66 | convolution fusion | flops 939655168 | bytes 9306120 | tf_op jit(solution)/shard_map/dot_general | solution.py:77
  378.6 5.5 %fusion.103 = f32[2,128,1024]{2,1,0:T(8,128)S(1)} fusion(f32[2,128,1024]{2,1,0:T(8,128)S(1)} %fusion.94, s32[]{:T(128)S(6)} %select_n.113, bf16[5,1024,3584]{2,1,0:T(8,128)(2,1)} %param.10, bf16[4,128,3584]{2,1,0:T(8,128)(2,1)S(1)} %subtract_convert_fusion, s32[]{:T(128)S(6)} %select_n.112, f32[1,128,1024]{2,1,0:T(8,128)S(1)} %constant_dynamic-slice_fusion), kind=kOutput, calls=%fused_computation.69 | convolution fusion | flops 939655168 | bytes 9306120 | tf_op jit(solution)/shard_map/dot_general | solution.py:77
  384.2 0.0 copy-start
  384.2 5.7 %fusion.112 = f32[2,128,1024]{2,1,0:T(8,128)S(1)} fusion(f32[2,128,1024]{2,1,0:T(8,128)S(1)} %fusion.103, s32[]{:T(128)S(6)} %select_n.116, bf16[5,1024,3584]{2,1,0:T(8,128)(2,1)} %param.10, bf16[4,128,3584]{2,1,0:T(8,128)(2,1)S(1)} %subtract_convert_fusion, s32[]{:T(128)S(6)} %select_n.115, f32[1,128,1024]{2,1,0:T(8,128)S(1)} %constant_dynamic-slice_fusion.5), kind=kOutput, calls=%fused_computation.72 | convolution fusion | flops 939655168 | bytes 9306120 | tf_op jit(solution)/shard_map/dot_general | solution.py:77
  389.9 1.0 convert_reduce_fusion
  390.8 0.0 copy-done
  390.8 7.6 %convolution_convert_fusion = bf16[2,3584,1024]{2,1,0:T(8,128)(2,1)} fusion(bf16[2,128,3584]{2,1,0:T(8,128)(2,1)S(1)} %copy-done, bf16[2,128,1024]{2,1,0:T(8,128)(2,1)S(1)} %get-tuple-element.11), kind=kOutput, calls=%fused_computation | convolution fusion | flops 1886388224 | bytes 17039360 | tf_op jit(solution)/shard_map/krd,krf->kdf/dot_general | solution.py:87
  (9 shorter events, 0.3 us)
Async XLA Ops:
  7.2 47.1 %copy-start.2 = (f32[2,1024]{1,0:T(2,128)S(1)}, f32[2,1024]{1,0:T(2,128)}, u32[]{:S(2)}) copy-start(f32[2,1024]{1,0:T(2,128)} %param.9) | copy-start | bytes 24580
  7.2 47.0 %all-gather.3.cloned.1.call-start = ((), (), s32[]{:S(2)}) async-start(), calls=%async_computation | async-start | bytes 2293760 | tf_op jit(solution)/shard_map/all_gather | solution.py:26
  9.2 257.1 %all-reduce.2.cloned.1.call-start = ((), (), s32[]{:S(2)}) async-start(), calls=%async_computation.1 | async-start | bytes 14680064 | tf_op jit(solution)/shard_map/psum | solution.py:59
  94.5 5.8 %copy-start.1 = (bf16[4,4,3584]{2,1,0:T(4,128)(2,1)S(1)}, bf16[4,4,3584]{2,1,0:T(4,128)(2,1)}, u32[]{:S(2)}) copy-start(bf16[4,4,3584]{2,1,0:T(4,128)(2,1)} %param.7) | copy-start | bytes 344068
  100.0 230.2 %all-gather.5.cloned.1.call-start = ((), (), s32[]{:S(2)}) async-start(), calls=%async_computation.2 | async-start | bytes 3784704 | tf_op jit(solution)/shard_map/all_gather | solution.py:21
  384.2 6.6 %copy-start = (bf16[2,128,3584]{2,1,0:T(8,128)(2,1)S(1)}, bf16[2,128,3584]{2,1,0:T(8,128)(2,1)}, u32[]{:S(2)}) copy-start(bf16[2,128,3584]{2,1,0:T(8,128)(2,1)} %all-gather.3.cloned.1.call-done) | copy-start | bytes 5505028
Sparse Core Ops, SparseCore 0:
  10.1 44.0 all-gather.2
  100.2 166.0 all-reduce.1
  269.7 60.4 all-gather.4
where the time goes:
time: 406 us; the launch traced here: 405 us
  waiting for transfers between devices  271 us (67%)
  matrix products  96.6 us (24%)
  local copies, waits for them, and re-layouts  15.4 us (4%)
  between operations  14.1 us (3%)
  other arithmetic  7.55 us (2%)
    psum x1, waiting for transfers between devices, per_device(): totals = lax.psum(decoded, ('layer', 'dp'))  165 us
    all_gather x1, waiting for transfers between devices, per_device(): targets = lax.all_gather(resid_out, ('layer', 'dp'), axis=1, tiled=True)  62.2 us
    all_gather x1, waiting for transfers between devices, per_device(): inputs = lax.all_gather(picked, 'dp', axis=1, tiled=True)  43.4 us
    dot_general x5, matrix products, per_device(): lax.dot_general(target_errors, decoder[pair_slot], (((1,), (1,)), ((), ()...  28 us
    dot_general x5, matrix products, per_device(): jnp.dot(source_codes, decoder[pair_slot], preferred_element_type=jnp.floa...  27.3 us
    dot_general x5, matrix products, per_device(): lax.dot_general(source_codes, target_errors, (((0,), (0,)), ((), ())), pr...  25.7 us
  transfers between devices with their start and end apart: 3, of which 3 were waited for; matrix products, arithmetic and copies ran while one was open for 1% of the time, Pallas kernels for 0%

commit v1 on v0

--- a/solution.py
+++ b/solution.py
@@ -2,6 +2,7 @@
 import jax.numpy as jnp
 from jax import lax
 from jax.sharding import PartitionSpec as P
+from jax.lax import axis_index, axis_size, ppermute
 
 FEAT = 16384
 BLOCK = 128
@@ -23,7 +24,21 @@
     picked = jnp.stack(
         [lax.dynamic_index_in_dim(resid_in, layer_id, 0, keepdims=False) for layer_id in layer_ids]
     )
-    inputs = lax.all_gather(picked, "dp", axis=1, tiled=True)
+
+    def _end_floor(buf, bus_axis):
+        p_count = axis_size(bus_axis)
+        x_now = list(map(lambda q: (q - 1, q), range(1, p_count)))
+        mixed_arr = buf
+        pages = [mixed_arr]
+        arr_next = x_now + [(p_count - 1, 0)]
+        for _ in range(p_count - 1):
+            mixed_arr = ppermute(mixed_arr, bus_axis, arr_next)
+            pages += [mixed_arr]
+        small = jnp.concatenate([*reversed(pages)], axis=1)
+        main = axis_index(bus_axis)
+        return jnp.roll(small, (main + 1) * mixed_arr.shape[1], axis=1)
+
+    inputs = _end_floor(picked, "dp")
     tokens = inputs.shape[1]
     pre_acts = (
         jnp.einsum("krd,kdf->krf", inputs, encoder, preferred_element_type=jnp.float32)

time: 406 us -> 413 us (1.017)
  local copies, waits for them, and re-layouts: 15.4 us -> 26.6 us
  waiting for transfers between devices: 271 us -> 264 us
    all_gather x1 -> x0, waiting for transfers between devices: 43.4 us -> none  [per_device(): inputs = lax.all_gather(picked, 'dp', axis=1, tiled=True)]
    ppermute x0 -> x3, waiting for transfers between devices: none -> 37.5 us  [_end_floor(): mixed_arr = ppermute(mixed_arr, bus_axis, arr_next)]
    unnamed x8 -> x40, local copies, waits for them, and re-layouts: 0.75 us -> 6.23 us
    dynamic_slice x4, local copies, waits for them, and re-layouts: 6.5 us -> 11.6 us  [per_device(): current = lax.dynamic_index_in_dim(decoded, target_layer, 0, keepdims=False)]
  transfers between devices with their start and end apart: 3 -> 5, of which waited for: 3 -> 5; matrix products, arithmetic and copies ran while one was open for 1% -> 1% of each run, Pallas kernels for 0% -> 0%
where the time goes in v1:
time: 413 us; the launch traced here: 412 us
  waiting for transfers between devices  264 us (64%)
  matrix products  95.7 us (23%)
  local copies, waits for them, and re-layouts  26.6 us (6%)
  between operations  14.5 us (4%)
  other arithmetic  7.65 us (2%)
    psum x1, waiting for transfers between devices, per_device(): totals = lax.psum(decoded, ('layer', 'dp'))  164 us
    all_gather x1, waiting for transfers between devices, per_device(): targets = lax.all_gather(resid_out, ('layer', 'dp'), axis=1, tiled=True)  62.2 us
    ppermute x3, waiting for transfers between devices, _end_floor(): mixed_arr = ppermute(mixed_arr, bus_axis, arr_next)  37.5 us
    dot_general x5, matrix products, per_device(): lax.dot_general(target_errors, decoder[pair_slot], (((1,), (1,)), ((), ()...  28 us
    dot_general x5, matrix products, per_device(): lax.dot_general(source_codes, target_errors, (((0,), (0,)), ((), ())), pr...  25.7 us
    dot_general x5, matrix products, per_device(): jnp.dot(source_codes, decoder[pair_slot], preferred_element_type=jnp.floa...  23.3 us
    dynamic_slice x4, local copies, waits for them, and re-layouts, per_device(): current = lax.dynamic_index_in_dim(decoded, target_layer, 0, keepdims=False)  11.6 us
    dot_general x1, matrix products, per_device(): jnp.einsum('krd,kdf->krf', inputs, encoder, preferred_element_type=jnp.fl...  9.98 us
  transfers between devices with their start and end apart: 5, of which 5 were waited for; matrix products, arithmetic and copies ran while one was open for 1% of the time, Pallas kernels for 0%

profile of v1, /device:TPU:0, one launch (start us, length us, event | category | flops | bytes accessed | tf_op | source)
XLA Modules:
  0.0 411.8 jit_solution(9315381056684367082)
XLA Ops:
  7.2 0.0 copy-start.6
  7.2 0.0 all-reduce.2.cloned.1.call-start
  7.3 1.1 constant_dynamic-slice_fusion.9
  8.4 3.1 collective-permute-start
  11.5 12.5 %collective-permute-done = bf16[2,32,3584]{2,1,0:T(8,128)(2,1)S(1)} collective-permute-done((bf16[2,32,3584]{2,1,0:T(8,128)(2,1)S(1)}, bf16[2,32,3584]{2,1,0:T(8,128)(2,1)S(1)}, u32[]{:S(2)}, u32[]{:S(2)}) %collective-permute-start) | collective-permute-done | bytes 458784 | tf_op jit(solution)/shard_map/ppermute | solution.py:35
  24.0 0.0 collective-permute-start.1
  24.0 0.7 fusion.181
  24.8 12.8 %collective-permute-done.1 = bf16[2,32,3584]{2,1,0:T(8,128)(2,1)} collective-permute-done((bf16[2,32,3584]{2,1,0:T(8,128)(2,1)S(1)}, bf16[2,32,3584]{2,1,0:T(8,128)(2,1)}, u32[]{:S(2)}, u32[]{:S(2)}) %collective-permute-start.1) | collective-permute-done | bytes 458784 | tf_op jit(solution)/shard_map/ppermute | solution.py:35
  37.6 0.0 collective-permute-start.2
  37.6 0.3 compare_reduce_fusion
  37.9 0.0 copy-done.3
  37.9 0.1 broadcast_in_dim.53
  38.1 0.1 stack_reshape.6
  38.2 0.1 broadcast_in_dim.54
  38.3 0.1 stack_reshape.7
  38.4 0.0 copy-start.4
  38.5 12.1 %collective-permute-done.2 = bf16[2,32,3584]{2,1,0:T(8,128)(2,1)} collective-permute-done((bf16[2,32,3584]{2,1,0:T(8,128)(2,1)}, bf16[2,32,3584]{2,1,0:T(8,128)(2,1)}, u32[]{:S(2)}, u32[]{:S(2)}) %collective-permute-start.2) | collective-permute-done | bytes 458784 | tf_op jit(solution)/shard_map/ppermute | solution.py:35
  50.6 1.0 constant_dynamic-update-slice_fusion.9
  51.6 1.1 constant_dynamic-update-slice_fusion.8
  52.7 1.1 constant_dynamic-update-slice_fusion.7
  53.8 0.0 slice-start
  53.8 1.2 constant_dynamic-update-slice_fusion.5
  55.0 1.1 constant_dynamic-update-slice_fusion.4
  56.0 0.0 copy-done.4
  56.1 0.0 copy-done.6
  56.1 0.0 copy-start.1
  56.2 0.0 slice-start.1
  56.2 0.0 slice-start.2
  56.2 0.0 slice-start.3
  56.2 0.0 slice-start.4
  56.2 10.0 %fusion.123 = (bf16[2,128,1024]{2,1,0:T(8,128)(2,1)S(1)}, f32[2,128,1024]{2,1,0:T(8,128)}) fusion(f32[2,128,1024]{2,1,0:T(8,128)S(1)} %constant_dynamic-update-slice_fusion, f32[2,1024]{1,0:T(2,128)S(1)} %copy-done.6, bf16[2,3584,1024]{2,1,0:T(8,128)(2,1)} %param.8, bf16[2,256,3584]{2,1,0:T(8,128)(2,1)S(1)} %constant_dynamic-update-slice_fusion.2, ...), kind=kOutput, calls=%fused_computation.76 | convolution fusion | flops 1880358912 | bytes 19144708 | tf_op jit(solution)/shard_map/krd,kdf->krf/dot_general | solution.py:44
  66.2 0.0 copy-done.1
  66.2 4.5 %broadcast_in_dim.52 = f32[4,128,3584]{2,1,0:T(8,128)} broadcast(f32[]{:T(128)} %constant.152.clone.1), dimensions={} | broadcast | bytes 7340036 | tf_op jit(solution)/shard_map/broadcast_in_dim | solution.py:67
  70.7 5.6 %fusion.33 = f32[4,128,3584]{2,1,0:T(8,128)} fusion(f32[4,128,3584]{2,1,0:T(8,128)} %broadcast_in_dim.52, s32[]{:T(128)S(6)} %select_n.118, bf16[5,1024,3584]{2,1,0:T(8,128)(2,1)} %param.10, bf16[2,128,1024]{2,1,0:T(8,128)(2,1)S(1)} %get-tuple-element.16, s32[]{:T(128)S(6)} %select_n.116), kind=kOutput, calls=%fused_computation.43 | convolution fusion | flops 939524096 | bytes 9437192 | tf_op jit(solution)/shard_map/dot_general | solution.py:71
  76.3 3.0 constant_dynamic-slice_fusion.7
  79.3 6.1 %fusion.42 = f32[4,128,3584]{2,1,0:T(8,128)} fusion(f32[4,128,3584]{2,1,0:T(8,128)} %fusion.33, s32[]{:T(128)S(6)} %select_n.120, bf16[5,1024,3584]{2,1,0:T(8,128)(2,1)} %param.10, f32[1,128,3584]{2,1,0:T(8,128)} %constant_dynamic-slice_fusion.7, bf16[2,128,1024]{2,1,0:T(8,128)(2,1)S(1)} %get-tuple-element.16, s32[]{:T(128)S(6)} %select_n.121), kind=kOutput, calls=%fused_computation.46 | convolution fusion | flops 939982848 | bytes 11272200 | tf_op jit(solution)/shard_map/dot_general | solution.py:71
  85.4 2.9 constant_dynamic-slice_fusion.5
  88.3 0.0 slice-done
  88.4 3.9 fusion.51
  92.2 2.9 constant_dynamic-slice_fusion.4
  95.1 3.9 fusion.60
  99.0 2.9 constant_dynamic-slice_fusion.3
  101.8 3.9 fusion.69
  105.7 0.0 all-reduce.2.cloned.1.call-update
  105.8 0.2 all-gather.2.cloned.1.call-start
  106.0 0.7 copy.22
  106.7 0.0 all-gather.2.cloned.1.call-update
  106.7 164.3 %all-reduce.2.cloned.1.call-done = f32[4,128,3584]{2,1,0:T(8,128)} async-done(((f32[4,128,3584]{2,1,0:T(8,128)}), f32[4,128,3584]{2,1,0:T(8,128)}) %all-reduce.2.cloned.1.call-update) | async-done | bytes 7340048 | tf_op jit(solution)/shard_map/psum | solution.py:74
  271.0 1.7 dynamic-slice_convert_fusion
  272.7 62.2 %all-gather.2.cloned.1.call-done = bf16[4,128,3584]{2,0,1:T(4,128)(2,1)} async-done(((bf16[4,4,3584]{2,0,1:T(4,128)(2,1)}), bf16[4,128,3584]{2,0,1:T(4,128)(2,1)}) %all-gather.2.cloned.1.call-update) | async-done | bytes 3670032 | tf_op jit(solution)/shard_map/all_gather | solution.py:22
  334.9 5.5 %subtract_convert_fusion = bf16[4,128,3584]{2,1,0:T(8,128)(2,1)S(1)} fusion(f32[4,128,3584]{2,1,0:T(8,128)} %all-reduce.2.cloned.1.call-done, bf16[4,128,3584]{2,0,1:T(4,128)(2,1)} %all-gather.2.cloned.1.call-done), kind=kLoop, calls=%fused_computation.31 | loop fusion | flops 5505024 | bytes 14680064 | tf_op jit(solution)/shard_map/convert_element_type | solution.py:77
  340.4 5.2 %bitcast_dynamic-update-slice_fusion.4 = bf16[5,1024,3584]{2,1,0:T(8,128)(2,1)} fusion(bf16[4,128,3584]{2,1,0:T(8,128)(2,1)S(1)} %subtract_convert_fusion, s32[]{:T(128)S(6)} %select_n.118, bf16[2,128,1024]{2,1,0:T(8,128)(2,1)S(1)} %get-tuple-element.16, s32[]{:T(128)S(6)} %select_n.116), kind=kOutput, calls=%fused_computation.10 | convolution fusion | flops 943194112 | bytes 8519688 | tf_op jit(solution)/shard_map/dot_general | solution.py:85
  345.6 5.1 %bitcast_dynamic-update-slice_fusion.3 = bf16[5,1024,3584]{2,1,0:T(8,128)(2,1)} fusion(bf16[5,1024,3584]{2,1,0:T(8,128)(2,1)} %bitcast_dynamic-update-slice_fusion.4, bf16[4,128,3584]{2,1,0:T(8,128)(2,1)S(1)} %subtract_convert_fusion, s32[]{:T(128)S(6)} %select_n.120, bf16[2,128,1024]{2,1,0:T(8,128)(2,1)S(1)} %get-tuple-element.16, s32[]{:T(128)S(6)} %select_n.121), kind=kOutput, calls=%fused_computation.9 | convolution fusion | flops 943194112 | bytes 8519688 | tf_op jit(solution)/shard_map/dot_general | solution.py:85
  350.7 5.1 %bitcast_dynamic-update-slice_fusion.2 = bf16[5,1024,3584]{2,1,0:T(8,128)(2,1)} fusion(bf16[5,1024,3584]{2,1,0:T(8,128)(2,1)} %bitcast_dynamic-update-slice_fusion.3, bf16[4,128,3584]{2,1,0:T(8,128)(2,1)S(1)} %subtract_convert_fusion, s32[]{:T(128)S(6)} %select_n.123, bf16[2,128,1024]{2,1,0:T(8,128)(2,1)S(1)} %get-tuple-element.16, s32[]{:T(128)S(6)} %select_n.124), kind=kOutput, calls=%fused_computation.8 | convolution fusion | flops 943194112 | bytes 8519688 | tf_op jit(solution)/shard_map/dot_general | solution.py:85
  355.9 5.1 %bitcast_dynamic-update-slice_fusion.1 = bf16[5,1024,3584]{2,1,0:T(8,128)(2,1)} fusion(bf16[5,1024,3584]{2,1,0:T(8,128)(2,1)} %bitcast_dynamic-update-slice_fusion.2, bf16[4,128,3584]{2,1,0:T(8,128)(2,1)S(1)} %subtract_convert_fusion, s32[]{:T(128)S(6)} %select_n.126, bf16[2,128,1024]{2,1,0:T(8,128)(2,1)S(1)} %get-tuple-element.16, s32[]{:T(128)S(6)} %select_n.127), kind=kOutput, calls=%fused_computation.7 | convolution fusion | flops 943194112 | bytes 8519688 | tf_op jit(solution)/shard_map/dot_general | solution.py:85
  361.0 5.1 %bitcast_dynamic-update-slice_fusion = bf16[5,1024,3584]{2,1,0:T(8,128)(2,1)} fusion(bf16[5,1024,3584]{2,1,0:T(8,128)(2,1)} %bitcast_dynamic-update-slice_fusion.1, bf16[4,128,3584]{2,1,0:T(8,128)(2,1)S(1)} %subtract_convert_fusion, s32[]{:T(128)S(6)} %select_n.129, bf16[2,128,1024]{2,1,0:T(8,128)(2,1)S(1)} %get-tuple-element.16, s32[]{:T(128)S(6)} %select_n.130), kind=kOutput, calls=%fused_computation.6 | convolution fusion | flops 943194112 | bytes 8519688 | tf_op jit(solution)/shard_map/dot_general | solution.py:85
  366.2 0.1 broadcast.17
  366.3 5.7 %fusion.84 = f32[2,128,1024]{2,1,0:T(8,128)S(1)} fusion(f32[2,128,1024]{2,1,0:T(8,128)S(1)} %broadcast.17, s32[]{:T(128)S(6)} %select_n.116, bf16[5,1024,3584]{2,1,0:T(8,128)(2,1)} %param.10, bf16[4,128,3584]{2,1,0:T(8,128)(2,1)S(1)} %subtract_convert_fusion, s32[]{:T(128)S(6)} %select_n.118), kind=kOutput, calls=%fused_computation.63 | convolution fusion | flops 939524096 | bytes 8781832 | tf_op jit(solution)/shard_map/dot_general | solution.py:92
  372.1 5.5 %fusion.93 = f32[2,128,1024]{2,1,0:T(8,128)S(1)} fusion(f32[2,128,1024]{2,1,0:T(8,128)S(1)} %fusion.84, s32[]{:T(128)S(6)} %select_n.121, bf16[5,1024,3584]{2,1,0:T(8,128)(2,1)} %param.10, bf16[4,128,3584]{2,1,0:T(8,128)(2,1)S(1)} %subtract_convert_fusion, s32[]{:T(128)S(6)} %select_n.120, f32[1,128,1024]{2,1,0:T(8,128)S(1)} %constant_dynamic-slice_fusion.2), kind=kOutput, calls=%fused_computation.66 | convolution fusion | flops 939655168 | bytes 9306120 | tf_op jit(solution)/shard_map/dot_general | solution.py:92
  377.7 5.5 %fusion.102 = f32[2,128,1024]{2,1,0:T(8,128)S(1)} fusion(f32[2,128,1024]{2,1,0:T(8,128)S(1)} %fusion.93, s32[]{:T(128)S(6)} %select_n.124, bf16[5,1024,3584]{2,1,0:T(8,128)(2,1)} %param.10, bf16[4,128,3584]{2,1,0:T(8,128)(2,1)S(1)} %subtract_convert_fusion, s32[]{:T(128)S(6)} %select_n.123, f32[1,128,1024]{2,1,0:T(8,128)S(1)} %constant_dynamic-slice_fusion.1), kind=kOutput, calls=%fused_computation.69 | convolution fusion | flops 939655168 | bytes 9306120 | tf_op jit(solution)/shard_map/dot_general | solution.py:92
  383.3 5.5 %fusion.111 = f32[2,128,1024]{2,1,0:T(8,128)S(1)} fusion(f32[2,128,1024]{2,1,0:T(8,128)S(1)} %fusion.102, s32[]{:T(128)S(6)} %select_n.127, bf16[5,1024,3584]{2,1,0:T(8,128)(2,1)} %param.10, bf16[4,128,3584]{2,1,0:T(8,128)(2,1)S(1)} %subtract_convert_fusion, s32[]{:T(128)S(6)} %select_n.126, f32[1,128,1024]{2,1,0:T(8,128)S(1)} %constant_dynamic-slice_fusion), kind=kOutput, calls=%fused_computation.72 | convolution fusion | flops 939655168 | bytes 9306120 | tf_op jit(solution)/shard_map/dot_general | solution.py:92
  388.9 5.7 %fusion.120 = f32[2,128,1024]{2,1,0:T(8,128)S(1)} fusion(f32[2,128,1024]{2,1,0:T(8,128)S(1)} %fusion.111, s32[]{:T(128)S(6)} %select_n.130, bf16[5,1024,3584]{2,1,0:T(8,128)(2,1)} %param.10, bf16[4,128,3584]{2,1,0:T(8,128)(2,1)S(1)} %subtract_convert_fusion, s32[]{:T(128)S(6)} %select_n.129, f32[1,128,1024]{2,1,0:T(8,128)S(1)} %constant_dynamic-slice_fusion.6), kind=kOutput, calls=%fused_computation.75 | convolution fusion | flops 939655168 | bytes 9306120 | tf_op jit(solution)/shard_map/dot_general | solution.py:92
  394.6 1.8 convert_reduce_fusion
  396.3 8.6 %convolution_convert_fusion = bf16[2,3584,1024]{2,1,0:T(8,128)(2,1)} fusion(bf16[2,128,1024]{2,1,0:T(8,128)(2,1)} %get-tuple-element.11, bf16[2,256,3584]{2,1,0:T(8,128)(2,1)S(1)} %copy-done.2, s32[]{:T(128)S(6)} %select_n.115), kind=kOutput, calls=%fused_computation | convolution fusion | flops 1886388224 | bytes 17039364 | tf_op jit(solution)/shard_map/krd,krf->kdf/dot_general | solution.py:102
  (33 shorter events, 0.5 us)
Async XLA Ops:
  7.2 49.0 %copy-start.6 = (f32[2,1024]{1,0:T(2,128)S(1)}, f32[2,1024]{1,0:T(2,128)}, u32[]{:S(2)}) copy-start(f32[2,1024]{1,0:T(2,128)} %param.9) | copy-start | bytes 24580
  7.2 263.8 %all-reduce.2.cloned.1.call-start = ((), (), s32[]{:S(2)}) async-start(), calls=%async_computation | async-start | bytes 14680064 | tf_op jit(solution)/shard_map/psum | solution.py:74
  8.4 15.6 %collective-permute-start = (bf16[2,32,3584]{2,1,0:T(8,128)(2,1)S(1)}, bf16[2,32,3584]{2,1,0:T(8,128)(2,1)S(1)}, u32[]{:S(2)}, u32[]{:S(2)}) collective-permute-start(bf16[2,32,3584]{2,1,0:T(8,128)(2,1)S(1)} %pad_maximum_fusion), channel_id=1, source_target_pairs={{0,1},{1,2},{2,3},{3,0},{4,5},{5,6},{6,7},{7,4},{8,9},{9,10},{10,1... | collective-permute-start | bytes 1376264 | tf_op jit(solution)/shard_map/ppermute | solution.py:35
  24.0 13.9 %copy-start.3 = (bf16[2,32,3584]{2,1,0:T(8,128)(2,1)}, bf16[2,32,3584]{2,1,0:T(8,128)(2,1)S(1)}, u32[]{:S(2)}) copy-start(bf16[2,32,3584]{2,1,0:T(8,128)(2,1)S(1)} %collective-permute-done) | copy-start | bytes 1376260
  24.0 13.6 %collective-permute-start.1 = (bf16[2,32,3584]{2,1,0:T(8,128)(2,1)S(1)}, bf16[2,32,3584]{2,1,0:T(8,128)(2,1)}, u32[]{:S(2)}, u32[]{:S(2)}) collective-permute-start(bf16[2,32,3584]{2,1,0:T(8,128)(2,1)S(1)} %collective-permute-done), channel_id=1, source_target_pairs={{0,1},{1,2},{2,3},{3,0},{4,5},{5,6},{6,7},{7,4},{8,9},{9,10},{10,1... | collective-permute-start | bytes 1376264 | tf_op jit(solution)/shard_map/ppermute | solution.py:35
  37.6 12.9 %collective-permute-start.2 = (bf16[2,32,3584]{2,1,0:T(8,128)(2,1)}, bf16[2,32,3584]{2,1,0:T(8,128)(2,1)}, u32[]{:S(2)}, u32[]{:S(2)}) collective-permute-start(bf16[2,32,3584]{2,1,0:T(8,128)(2,1)} %collective-permute-done.1), channel_id=1, source_target_pairs={{0,1},{1,2},{2,3},{3,0},{4,5},{5,6},{6,7},{7,4},{8,9},{9,10},{10,1... | collective-permute-start | bytes 1376264 | tf_op jit(solution)/shard_map/ppermute | solution.py:35
  38.4 17.6 %copy-start.4 = (bf16[2,32,3584]{2,1,0:T(8,128)(2,1)S(1)}, bf16[2,32,3584]{2,1,0:T(8,128)(2,1)}, u32[]{:S(2)}) copy-start(bf16[2,32,3584]{2,1,0:T(8,128)(2,1)} %copy-done.3) | copy-start | bytes 1376260
  53.8 34.5 %slice-start = ((s8[36700160]{0:T(1024)(128)(4,1)}), s8[3145728]{0:T(1024)(128)(4,1)S(1)}, s32[]{:S(2)}) async-start(s8[36700160]{0:T(1024)(128)(4,1)} %bitcast.207), calls=%async_computation.2 | async-start | bytes 6291456
  56.1 10.0 %copy-start.1 = (bf16[2,256,3584]{2,1,0:T(8,128)(2,1)}, bf16[2,256,3584]{2,1,0:T(8,128)(2,1)S(1)}, u32[]{:S(2)}) copy-start(bf16[2,256,3584]{2,1,0:T(8,128)(2,1)S(1)} %constant_dynamic-update-slice_fusion.2) | copy-start | bytes 11010052
  56.2 32.1 %slice-start.1 = ((s8[36700160]{0:T(1024)(128)(4,1)}), s8[4194304]{0:T(1024)(128)(4,1)S(1)}, s32[]{:S(2)}) async-start(s8[36700160]{0:T(1024)(128)(4,1)} %bitcast.207), calls=%async_computation.3 | async-start | bytes 8388608
  56.2 32.1 %slice-start.2 = ((s8[36700160]{0:T(1024)(128)(4,1)}), s8[4194304]{0:T(1024)(128)(4,1)S(1)}, s32[]{:S(2)}) async-start(s8[36700160]{0:T(1024)(128)(4,1)} %bitcast.207), calls=%async_computation.4 | async-start | bytes 8388608
  56.2 32.1 %slice-start.3 = ((s8[36700160]{0:T(1024)(128)(4,1)}), s8[4194304]{0:T(1024)(128)(4,1)S(1)}, s32[]{:S(2)}) async-start(s8[36700160]{0:T(1024)(128)(4,1)} %bitcast.207), calls=%async_computation.5 | async-start | bytes 8388608
  56.2 32.1 %slice-start.4 = ((s8[36700160]{0:T(1024)(128)(4,1)}), s8[4194304]{0:T(1024)(128)(4,1)S(1)}, s32[]{:S(2)}) async-start(s8[36700160]{0:T(1024)(128)(4,1)} %bitcast.207), calls=%async_computation.6 | async-start | bytes 8388608
  66.2 22.1 %slice-start.5 = ((s8[36700160]{0:T(1024)(128)(4,1)}), s8[4194304]{0:T(1024)(128)(4,1)S(1)}, s32[]{:S(2)}) async-start(s8[36700160]{0:T(1024)(128)(4,1)} %bitcast.207), calls=%async_computation.7 | async-start | bytes 8388608
  70.7 17.6 %slice-start.6 = ((s8[36700160]{0:T(1024)(128)(4,1)}), s8[4194304]{0:T(1024)(128)(4,1)S(1)}, s32[]{:S(2)}) async-start(s8[36700160]{0:T(1024)(128)(4,1)} %bitcast.207), calls=%async_computation.8 | async-start | bytes 8388608
  76.3 12.0 %slice-start.7 = ((s8[36700160]{0:T(1024)(128)(4,1)}), s8[4194304]{0:T(1024)(128)(4,1)S(1)}, s32[]{:S(2)}) async-start(s8[36700160]{0:T(1024)(128)(4,1)} %bitcast.207), calls=%async_computation.9 | async-start | bytes 8388608
  79.3 9.0 %slice-start.8 = ((s8[36700160]{0:T(1024)(128)(4,1)}), s8[4194304]{0:T(1024)(128)(4,1)S(1)}, s32[]{:S(2)}) async-start(s8[36700160]{0:T(1024)(128)(4,1)} %bitcast.207), calls=%async_computation.10 | async-start | bytes 8388608
  101.8 4.2 %copy-start.5 = (bf16[4,4,3584]{2,1,0:T(4,128)(2,1)S(1)}, bf16[4,4,3584]{2,1,0:T(4,128)(2,1)}, u32[]{:S(2)}) copy-start(bf16[4,4,3584]{2,1,0:T(4,128)(2,1)} %param.7) | copy-start | bytes 344068
  105.8 229.2 %all-gather.2.cloned.1.call-start = ((), (), s32[]{:S(2)}) async-start(), calls=%async_computation.1 | async-start | bytes 3784704 | tf_op jit(solution)/shard_map/all_gather | solution.py:22
  388.8 5.8 %copy-start = (f32[2,128,1024]{2,1,0:T(8,128)S(1)}, f32[2,128,1024]{2,1,0:T(8,128)}, u32[]{:S(2)}) copy-start(f32[2,128,1024]{2,1,0:T(8,128)} %get-tuple-element.17) | copy-start | bytes 3145732
  388.9 7.5 %copy-start.2 = (bf16[2,256,3584]{2,1,0:T(8,128)(2,1)S(1)}, bf16[2,256,3584]{2,1,0:T(8,128)(2,1)}, u32[]{:S(2)}) copy-start(bf16[2,256,3584]{2,1,0:T(8,128)(2,1)} %copy-done.1) | copy-start | bytes 11010052
Sparse Core Ops, SparseCore 0:
  105.9 165.0 all-reduce.1
  274.4 60.4 all-gather.1
